TPU v7x, 256 devices: a whole 4x4x8 slice. The times are simulated.
256 devices in a mesh: dp: 4 (over x), seq: 64 (over z, y, core).
Axes of the slice: x: 4, y: 4, z: 8, core: 2. Of those that a mesh axis runs over, the one named last changes fastest.
Arguments:
- streams: bfloat16 [3, 4, 8192, 4096], P(None, 'dp', 'seq'), may hold values from -6 to 6
- short_filter: float32 [3, 3, 4096], P(None, None, 'dp'), may hold values from -3.5 to 3.5
- decay_rate: float32 [2, 4096], P(None, 'dp'), may hold values from 1.2207031e-06 to 0.05
- pole_angle: float32 [2, 4096], P(None, 'dp'), may hold values from -3.140625 to 3.140625
- residue_re: float32 [2, 4096], P(None, 'dp'), may hold values from -6 to 6
- residue_im: float32 [2, 4096], P(None, 'dp'), may hold values from -6 to 6
- skip_gain: float32 [4096], P('dp'), may hold values from -6 to 6
- doc_starts: int32 [4, 8], P('dp'), may hold values from 0 to 8191, as said below
Outputs:
- mixed: bfloat16 [4, 8192, 4096], P('dp', 'seq')
Inputs may be any that keep to these rules, and one draw needn't show every extreme that they name: `doc_starts`: each row starts with 0 and rises strictly; the last document of every sequence is one position long.
All inputs are finite; a program needn't handle non-finite values.
Results may differ from a plain program's by a relative error of at most 0.0045.
Values may be sent and summed in bfloat16 or wider, within the bound.
A program may use at most 128 MiB of HBM per device.

v0:
```python
import jax
import jax.numpy as jnp
from jax import lax
from jax.sharding import PartitionSpec as P

block_len = 32


def from_behind(x, axis, by):
    count = lax.axis_size(axis)
    pairs = [(i, i + by) for i in range(count) if 0 <= i + by < count]
    return lax.ppermute(x, axis, pairs)


def prefix_2(part, axis, combine, identity):
    place = lax.axis_index(axis)
    gathered = jax.tree.map(lambda a: lax.all_gather(a, axis), part)
    state = jax.tree.map(lambda a, e: jnp.zeros_like(a) + jnp.asarray(e, a.dtype), part, identity)

    def one(turn, state):
        return combine(
            state, jax.tree.map(lambda a: lax.dynamic_index_in_dim(a, turn, 0, False), gathered)
        )

    return lax.fori_loop(0, place, one, state)


def pole_power(decay, rotation, powers):
    magnitude = jnp.exp(-decay * powers)
    return (magnitude * jnp.cos(rotation * powers), magnitude * jnp.sin(rotation * powers))


def segment_of(positions, starts):
    return jnp.sum((positions[..., None] >= starts).astype(jnp.int32), axis=-1) - 1


def local(
    streams, short_filter, decay_rate, pole_angle, residue_re, residue_im, skip_gain, doc_starts
):
    short_filter, decay_rate, pole_angle, residue_re, residue_im, skip_gain = (
        lax.all_gather(short_filter, "dp", axis=2, tiled=True),
        lax.all_gather(decay_rate, "dp", axis=1, tiled=True),
        lax.all_gather(pole_angle, "dp", axis=1, tiled=True),
        lax.all_gather(residue_re, "dp", axis=1, tiled=True),
        lax.all_gather(residue_im, "dp", axis=1, tiled=True),
        lax.all_gather(skip_gain, "dp", axis=0, tiled=True),
    )
    tok_rows = streams.shape[2]
    channels = streams.shape[3]
    modes = decay_rate.shape[0]
    my_index = lax.axis_index("seq")
    offset = my_index * tok_rows
    starts = doc_starts[0]
    rim_rows = streams[:, :, tok_rows - 2 :, :]
    before = from_behind(rim_rows, "seq", 1)
    extended = jnp.concatenate([before, streams], axis=2)[:, 0]
    filtered = (
        short_filter[0][:, None, :] * extended[:, 2:]
        + short_filter[1][:, None, :] * extended[:, 1:-1]
        + short_filter[2][:, None, :] * extended[:, :-2]
    )
    product = filtered[0] * filtered[1]
    out_gate = filtered[2]
    positions = offset + jnp.arange(tok_rows, dtype=jnp.int32)
    seg_ids = segment_of(positions, starts)
    seg_before = segment_of(offset - 1 + jnp.zeros((1,), jnp.int32), starts)[0]
    nblocks = tok_rows // block_len
    local_steps = jnp.arange(block_len, dtype=jnp.float32)[:, None, None]
    fwd_re, fwd_im = pole_power(decay_rate, pole_angle, local_steps)
    back_re, back_im = pole_power(-decay_rate, -pole_angle, local_steps)
    blocked = product.reshape(nblocks, block_len, 1, channels)
    lifted = jnp.concatenate([blocked * back_re, blocked * back_im], axis=2)
    lifted = lifted.reshape(nblocks, block_len, 2 * modes * channels)
    seg_blocks = seg_ids.reshape(nblocks, block_len)
    causal = jnp.arange(block_len)[:, None] >= jnp.arange(block_len)[None, :]
    within = (causal[None] & (seg_blocks[:, :, None] == seg_blocks[:, None, :])).astype(jnp.float32)
    summed = jnp.einsum("bts,bsk->btk", within, lifted, precision=lax.Precision.HIGHEST)
    summed = summed.reshape(nblocks, block_len, 2 * modes, channels)
    sum_re = summed[:, :, :modes]
    sum_im = summed[:, :, modes:]
    state_re = fwd_re * sum_re - fwd_im * sum_im
    state_im = fwd_re * sum_im + fwd_im * sum_re
    step_re, step_im = pole_power(decay_rate, pole_angle, jnp.float32(block_len))
    entry_seg = jnp.concatenate([seg_before[None], seg_blocks[:-1, -1]])
    keeps_last = (seg_blocks[:, -1] == entry_seg).astype(jnp.float32)

    def advance(running, inputs):
        run_re, run_im = running
        last_re, last_im, kept_now = inputs
        next_re = last_re + kept_now * (step_re * run_re - step_im * run_im)
        next_im = last_im + kept_now * (step_re * run_im + step_im * run_re)
        return ((next_re, next_im), (run_re, run_im))

    zero_state = jnp.zeros((modes, channels), jnp.float32)
    (end_re, end_im), (entry_re, entry_im) = lax.scan(
        advance, (zero_state, zero_state), (state_re[:, -1], state_im[:, -1], keeps_last)
    )
    lead_re, lead_im = pole_power(decay_rate, pole_angle, local_steps + 1.0)
    joined = (seg_blocks == entry_seg[:, None]).astype(jnp.float32)[:, :, None, None]
    state_re = state_re + joined * (lead_re * entry_re[:, None] - lead_im * entry_im[:, None])
    state_im = state_im + joined * (lead_re * entry_im[:, None] + lead_im * entry_re[:, None])
    whole_re, whole_im = pole_power(decay_rate, pole_angle, jnp.float32(tok_rows))
    keep_all = (seg_ids[-1] == seg_before).astype(jnp.float32)

    def combine(earlier, latter):
        early_are, early_aim, early_sre, early_sim = earlier
        late_are, late_aim, late_sre, late_sim = latter
        return (
            late_are * early_are - late_aim * early_aim,
            late_are * early_aim + late_aim * early_are,
            late_sre + late_are * early_sre - late_aim * early_sim,
            late_sim + late_are * early_sim + late_aim * early_sre,
        )

    unit_state = jnp.ones_like(end_re)
    prefix = prefix_2(
        (keep_all * whole_re, keep_all * whole_im, end_re, end_im),
        "seq",
        combine,
        (unit_state, zero_state, zero_state, zero_state),
    )
    inflow_re = prefix[2]
    inflow_im = prefix[3]
    all_steps = (
        jnp.arange(tok_rows, dtype=jnp.float32).reshape(nblocks, block_len)[:, :, None, None] + 1.0
    )
    enter_re, enter_im = pole_power(decay_rate, pole_angle, all_steps)
    reach = (seg_blocks == seg_before).astype(jnp.float32)[:, :, None, None]
    state_re = state_re + reach * (enter_re * inflow_re - enter_im * inflow_im)
    state_im = state_im + reach * (enter_re * inflow_im + enter_im * inflow_re)
    norm_factor = jnp.sqrt(-jnp.expm1(-2.0 * decay_rate))
    long_part = jnp.sum(norm_factor * (residue_re * state_re - residue_im * state_im), axis=2)
    long_part = long_part.reshape(tok_rows, channels)
    response = skip_gain * product + long_part
    return (out_gate * response).astype(jnp.bfloat16)[None]


def solution(mesh):
    placed = (
        P(None, "dp", "seq", None),
        P(None, None, "dp"),
        P(None, "dp"),
        P(None, "dp"),
        P(None, "dp"),
        P(None, "dp"),
        P("dp"),
        P("dp", None),
    )
    return jax.shard_map(
        local, mesh=mesh, in_specs=placed, out_specs=P("dp", "seq", None), check_vma=False
    )
```

profile of v0, /device:TPU:249, one launch (start us, length us, event | category | flops | bytes accessed | tf_op | source)
XLA Modules:
  0.0 430.3 jit_solution(6064338715635104115)
XLA Ops:
  6.5 1.3 fusion.14
  10.5 9.6 %all_gather.46 = f32[2,4096]{1,0:T(2,128)S(1)} all-gather(f32[2,1024]{1,0:T(2,128)} %param.15), channel_id=1, replica_groups=mesh['dp'=4,'seq'=64] {'dp'}, dimensions={1}, use_global_device_ids=true | all-gather | bytes 40960 | tf_op jit(solution)/shard_map/all_gather | solution.py:43
  20.1 9.2 %all_gather.44 = f32[2,4096]{1,0:T(2,128)S(1)} all-gather(f32[2,1024]{1,0:T(2,128)} %param.14), channel_id=1, replica_groups=mesh['dp'=4,'seq'=64] {'dp'}, dimensions={1}, use_global_device_ids=true | all-gather | bytes 40960 | tf_op jit(solution)/shard_map/all_gather | solution.py:42
  29.3 1.7 multiply_bitcast_fusion
  31.0 1.0 slice.69
  32.0 1.3 collective-permute-start
  33.8 16.3 %cosine_multiply_fusion = (f32[32,2,4096]{2,1,0:T(2,128)}, f32[32,2,4096]{2,1,0:T(2,128)}) fusion(f32[2,4096]{1,0:T(2,128)S(1)} %get-tuple-element.233, f32[2,4096]{1,0:T(2,128)S(1)} %all_gather.44), kind=kLoop, calls=%fused_computation.37 | loop fusion | flops 1048576 | bytes 2162688 | tf_op jit(solution)/shard_map/mul | solution.py:30
  50.2 9.8 %all_gather.42 = f32[3,3,4096]{2,1,0:T(4,128)S(1)} all-gather(f32[3,3,1024]{2,1,0:T(4,128)} %param.13), channel_id=1, replica_groups=mesh['dp'=4,'seq'=64] {'dp'}, dimensions={2}, use_global_device_ids=true | all-gather | bytes 184320 | tf_op jit(solution)/shard_map/all_gather | solution.py:41
  60.0 8.6 %fusion.6 = (f32[32,2,4096]{2,0,1:T(8,128)S(1)}, f32[32,2,4096]{2,0,1:T(8,128)S(1)}, f32[32,2,4096]{2,0,1:T(8,128)}, f32[32,2,4096]{2,0,1:T(8,128)}) fusion(f32[32]{0:T(128)S(1)} %iota_add_fusion, f32[2,4096]{1,0:T(2,128)S(1)} %all_gather.46, f32[2,4096]{1,0:T(2,128)S(1)} %get-tuple-element.234), kind=kLoop, calls=%fused_computation.32 | loop fusion | flops 2097152 | bytes 4259968 | tf_op jit(solution)/shard_map/mul | solution.py:30
  68.7 2.7 maximum_bitcast_fusion
  71.4 2.1 multiply_add_fusion
  73.8 1.7 copy-done.4
  75.6 1.1 copy-done.5
  76.7 3.9 broadcast_multiply_fusion.1
  80.5 9.7 %pad_maximum_fusion = f32[4,32,4,4096]{3,2,1,0:T(4,128)} fusion(f32[4,32,2,4096]{3,2,1,0:T(2,128)} %get-tuple-element.218, f32[4,32,2,4096]{3,2,1,0:T(2,128)S(1)} %get-tuple-element.217), kind=kLoop, calls=%fused_computation.14 | loop fusion | flops 2097152 | bytes 16777216 | tf_op jit(solution)/shard_map/concatenate | solution.py:72
  90.3 11.0 %reshape.158 = f32[4,32,16384]{2,1,0:T(8,128)} reshape(f32[4,32,4,4096]{3,2,1,0:T(4,128)} %pad_maximum_fusion) | data formatting | bytes 16777216 | tf_op jit(solution)/shard_map/reshape | solution.py:73
  101.3 10.8 %fusion.8 = f32[4,32,16384]{2,1,0:T(8,128)} fusion(f32[4,32,16384]{2,1,0:T(8,128)} %reshape.158, s32[4,32]{1,0:T(4,128)S(1)} %sub.35, pred[32,32]{1,0:T(8,128)(4,1)S(1)} %iota_compare_fusion), kind=kOutput, calls=%fused_computation.48 | convolution fusion | flops 805314560 | bytes 16778752 | tf_op jit(solution)/shard_map/bts,bsk->btk/dot_general | solution.py:77
  112.1 10.8 %reshape.159 = f32[4,32,4,4096]{3,2,1,0:T(4,128)} reshape(f32[4,32,16384]{2,1,0:T(8,128)} %fusion.8) | data formatting | bytes 16777216 | tf_op jit(solution)/shard_map/reshape | solution.py:78
  122.9 11.1 %fusion.15 = (f32[4,32,2,4096]{3,2,1,0:T(2,128)S(1)}, f32[4,32,2,4096]{3,2,1,0:T(2,128)}) fusion(f32[4,32,4,4096]{3,2,1,0:T(4,128)} %reshape.159), kind=kLoop, calls=%fused_computation.75 | loop fusion | bytes 16777216 | tf_op jit(solution)/shard_map/slice | solution.py:79
  134.0 7.8 %multiply_subtract_fusion = (f32[4,32,2,4096]{3,1,2,0:T(8,128)S(1)}, f32[4,32,2,4096]{3,1,2,0:T(8,128)S(1)}) fusion(f32[4,32,2,4096]{3,2,1,0:T(2,128)} %get-tuple-element.216, f32[4,32,2,4096]{3,2,1,0:T(2,128)S(1)} %get-tuple-element.215, f32[32,2,4096]{2,0,1:T(8,128)S(1)} %copy-done.3, f32[32,2,4096]{2,0,1:T(8,128)} %get-tuple-element.225), kind=kLoop, calls=%fused_computation.22 | loop fusion | flops 6291456 | bytes 18874368 | tf_op jit(solution)/shard_map/sub | solution.py:81
  141.9 2.0 copy-done.1
  144.0 1.1 copy-done.2
  145.5 7.9 %while.33 = (s32[]{:T(128)}, f32[2,4096]{1,0:T(2,128)S(1)}, f32[2,4096]{1,0:T(2,128)S(1)}, f32[4,2,4096]{2,1,0:T(2,128)S(1)}, f32[4,2,4096]{2,1,0:T(2,128)}, /*i...) while((s32[]{:T(128)}, f32[2,4096]{1,0:T(2,128)S(1)}, ...), condition=%wide.region_3.4_spmd.clone, body=%wide.region_2.3_spmd.clone.sunk | while | flops 114691 | bytes 393876 | solution.py:95
  154.6 9.0 %all_gather.43 = f32[4096]{0:T(1024)S(1)} all-gather(f32[1024]{0:T(1024)S(1)} %copy-done.10), channel_id=1, replica_groups=mesh['dp'=4,'seq'=64] {'dp'}, dimensions={0}, use_global_device_ids=true | all-gather | bytes 20480 | tf_op jit(solution)/shard_map/all_gather | solution.py:46
  163.7 9.6 %all_gather.45 = f32[2,4096]{1,0:T(2,128)S(1)} all-gather(f32[2,1024]{1,0:T(2,128)S(1)} %copy-done.8), channel_id=1, replica_groups=mesh['dp'=4,'seq'=64] {'dp'}, dimensions={1}, use_global_device_ids=true | all-gather | bytes 40960 | tf_op jit(solution)/shard_map/all_gather | solution.py:44
  173.2 9.0 %all_gather.55 = f32[2,4096]{1,0:T(2,128)S(1)} all-gather(f32[2,1024]{1,0:T(2,128)S(1)} %copy-done.9), channel_id=1, replica_groups=mesh['dp'=4,'seq'=64] {'dp'}, dimensions={1}, use_global_device_ids=true | all-gather | bytes 40960 | tf_op jit(solution)/shard_map/all_gather | solution.py:45
  182.4 6.7 %all-gather.17.cloned.1.call-done = f32[64,2,4096]{2,1,0:T(2,128)} async-done(((f32[1,2,4096]{2,1,0:T(2,128)}), f32[64,2,4096]{2,1,0:T(2,128)}) %all-gather.17.cloned.1.call-update) | async-done | bytes 2097168 | tf_op jit(solution)/shard_map/all_gather | solution.py:17
  189.1 77.8 %all-gather.13.cloned.1.call-done = f32[64,2,4096]{2,1,0:T(2,128)} async-done(((f32[1,2,4096]{2,1,0:T(2,128)}), f32[64,2,4096]{2,1,0:T(2,128)}) %all-gather.13.cloned.1.call-update) | async-done | bytes 2097168 | tf_op jit(solution)/shard_map/all_gather | solution.py:17
  266.9 77.6 %all-gather.19.cloned.1.call-done = f32[64,2,4096]{2,1,0:T(2,128)} async-done(((f32[1,2,4096]{2,1,0:T(2,128)}), f32[64,2,4096]{2,1,0:T(2,128)}) %all-gather.19.cloned.1.call-update) | async-done | bytes 2097168 | tf_op jit(solution)/shard_map/all_gather | solution.py:17
  344.5 56.3 %while.32 = (s32[]{:T(128)}, f32[2,4096]{1,0:T(2,128)S(1)}, f32[2,4096]{1,0:T(2,128)S(1)}, s32[]{:T(128)}, f32[64,2,4096]{2,1,0:T(2,128)}, /*index=5*/f32[64,2,4...) while((s32[]{:T(128)}, f32[2,4096]{1,0:T(2,128)S(1)}, ...), condition=%wide.region_5.6_spmd, body=%wide.region_4.5_spmd.sunk | while | flops 65541 | bytes 262291 | solution.py:25
  400.8 21.4 %multiply_reduce_fusion = f32[4,32,4096]{2,1,0:T(8,128)S(1)} fusion(f32[4,32,2,4096]{3,1,2,0:T(8,128)} %copy-done.2, f32[4,32,2,4096]{3,1,2,0:T(8,128)} %copy-done.1, f32[2,4096]{1,0:T(2,128)S(1)} %all_gather.55, f32[2,4096]{1,0:T(2,128)S(1)} %get-tuple-element.135, f32[2,4096]{1,0:T(2,128)S(1)} %get-tuple-element.134, f32[2,4096]{1,0:T(2,128)S(1)} %all_gather.46, ...), kind=kLoop, calls=%fused_computation.20 | loop fusion | flops 29884416 | bytes 13075968 | tf_op jit(solution)/shard_map/reduce_sum | solution.py:132
  422.2 1.6 fusion.5
  (131 shorter events, 66.7 us)
Async XLA Ops:
  6.5 175.8 %all-gather.15.cloned.1.call-start = ((), (), s32[]{:S(2)}) async-start(), calls=%async_computation.1 | async-start | bytes 2129920 | tf_op jit(solution)/shard_map/all_gather | solution.py:17
  31.0 158.1 %all-gather.17.cloned.1.call-start = ((), (), s32[]{:S(2)}) async-start(), calls=%async_computation.2 | async-start | bytes 2129920 | tf_op jit(solution)/shard_map/all_gather | solution.py:17
  32.0 36.7 %collective-permute-start = (bf16[3,1,2,4096]{3,2,0,1:T(2,128)(2,1)S(1)}, bf16[3,1,2,4096]{3,2,0,1:T(2,128)(2,1)S(1)}, u32[]{:S(2)}, u32[]{:S(2)}) collective-permute-start(bf16[3,1,2,4096]{3,2,0,1:T(2,128)(2,1)S(1)} %slice.69), channel_id=1, source_target_pairs={{0,1},{1,2},{2,3},{3,4},{4,5},{5,6},{6,7},{7,8},{8,9},{9,10},{10,1... | collective-permute-start | bytes 147464 | tf_op jit(solution)/shard_map/ppermute | solution.py:12
  33.3 233.5 %all-gather.13.cloned.1.call-start = ((), (), s32[]{:S(2)}) async-start(), calls=%async_computation | async-start | bytes 2129920 | tf_op jit(solution)/shard_map/all_gather | solution.py:17
  73.5 7.0 %copy-start = (f32[3,128,4096]{2,1,0:T(8,128)}, f32[3,128,4096]{2,1,0:T(8,128)S(1)}, u32[]{:S(2)}) copy-start(f32[3,128,4096]{2,1,0:T(8,128)S(1)} %multiply_add_fusion) | copy-start | bytes 18874372
  73.6 2.0 copy-start.4
  73.6 3.1 copy-start.5
  122.9 11.1 %copy-start.3 = (f32[32,2,4096]{2,0,1:T(8,128)S(1)}, f32[32,2,4096]{2,0,1:T(8,128)}, u32[]{:S(2)}) copy-start(f32[32,2,4096]{2,0,1:T(8,128)} %get-tuple-element.224) | copy-start | bytes 3145732
  134.0 20.6 %copy-start.10 = (f32[1024]{0:T(1024)S(1)}, f32[1024]{0:T(1024)}, u32[]{:S(2)}) copy-start(f32[1024]{0:T(1024)} %param.18) | copy-start | bytes 12292
  134.0 29.7 %copy-start.8 = (f32[2,1024]{1,0:T(2,128)S(1)}, f32[2,1024]{1,0:T(2,128)}, u32[]{:S(2)}) copy-start(f32[2,1024]{1,0:T(2,128)} %param.16) | copy-start | bytes 24580
  134.0 39.2 %copy-start.9 = (f32[2,1024]{1,0:T(2,128)S(1)}, f32[2,1024]{1,0:T(2,128)}, u32[]{:S(2)}) copy-start(f32[2,1024]{1,0:T(2,128)} %param.17) | copy-start | bytes 24580
  141.8 2.0 copy-start.1
  141.8 3.3 copy-start.2
  153.4 0.6 copy-start.6
  153.4 0.7 copy-start.7
  154.0 190.4 %all-gather.19.cloned.1.call-start = ((), (), s32[]{:S(2)}) async-start(), calls=%async_computation.3 | async-start | bytes 2129920 | tf_op jit(solution)/shard_map/all_gather | solution.py:17
  400.8 21.4 %slice-start = ((s8[6291456]{0:T(1024)(128)(4,1)}), s8[4194304]{0:T(1024)(128)(4,1)S(1)}, s32[]{:S(2)}) async-start(s8[6291456]{0:T(1024)(128)(4,1)} %bitcast.73), calls=%async_computation.4 | async-start | bytes 8388608
  400.8 21.4 %slice-start.1 = ((s8[6291456]{0:T(1024)(128)(4,1)}), s8[2097152]{0:T(1024)(128)(4,1)S(1)}, s32[]{:S(2)}) async-start(s8[6291456]{0:T(1024)(128)(4,1)} %bitcast.73), calls=%async_computation.5 | async-start | bytes 4194304
Sparse Core Ops, SparseCore 0:
  31.1 80.2 all-gather.14
  114.1 74.9 all-gather.16
  191.9 74.9 all-gather.12
  269.5 74.9 all-gather.18
where the time goes:
time: 436 us; the launch traced here: 430 us
  waiting for transfers between devices  163 us (37%)
  other arithmetic  139 us (32%)
  blocking collectives  56.2 us (13%)
  local copies, waits for them, and re-layouts  44.3 us (10%)
  between operations  14.7 us (3%)
  matrix products  10.8 us (2%)
    all_gather x4, waiting for transfers between devices, prefix_2(): gathered = jax.tree.map(lambda a: lax.all_gather(a, axis), part)  162 us
    add x63, other arithmetic, combine(): late_sim + late_are * early_sim + late_aim * early_sre  54.8 us
    mul x2, other arithmetic, pole_power(): magnitude * jnp.cos(rotation * powers)  24.9 us
    reduce_sum x1, other arithmetic, local(): jnp.sum(norm_factor * (residue_re * state_re - residue_im * state_im), ax...  21.4 us
    slice x1, local copies, waits for them, and re-layouts, local(): sum_re = summed[:, :, :modes]  11.1 us
    reshape x1, local copies, waits for them, and re-layouts, local(): lifted = lifted.reshape(nblocks, block_len, 2 * modes * channels)  11 us
    dot_general x1, matrix products, local(): jnp.einsum('bts,bsk->btk', within, lifted, precision=lax.Precision.HIGHEST)  10.8 us
    reshape x1, local copies, waits for them, and re-layouts, local(): summed = summed.reshape(nblocks, block_len, 2 * modes, channels)  10.8 us
  transfers between devices with their start and end apart: 5, of which 3 were waited for; matrix products, arithmetic and copies ran while one was open for 24% of the time, Pallas kernels for 0%

commit v1 on v0

--- a/solution.py
+++ b/solution.py
@@ -4,6 +4,13 @@
 from jax.sharding import PartitionSpec as P
 
 block_len = 32
+
+
+def swapped_in(shard, axis, dim):
+    size = lax.axis_size(axis)
+    parts = jnp.stack([shard for _ in range(size)])
+    parts = lax.all_to_all(parts, axis, split_axis=0, concat_axis=0)
+    return jnp.concatenate(parts, axis=dim)
 
 
 def from_behind(x, axis, by):
@@ -40,7 +47,7 @@
     short_filter, decay_rate, pole_angle, residue_re, residue_im, skip_gain = (
         lax.all_gather(short_filter, "dp", axis=2, tiled=True),
         lax.all_gather(decay_rate, "dp", axis=1, tiled=True),
-        lax.all_gather(pole_angle, "dp", axis=1, tiled=True),
+        swapped_in(pole_angle, "dp", 1),
         lax.all_gather(residue_re, "dp", axis=1, tiled=True),
         lax.all_gather(residue_im, "dp", axis=1, tiled=True),
         lax.all_gather(skip_gain, "dp", axis=0, tiled=True),

time: 436 us -> 430 us (0.986)
  blocking collectives: 56.2 us -> 47.2 us
    all_gather x1 -> x0, blocking collectives: 9.58 us -> none  [local(): lax.all_gather(pole_angle, 'dp', axis=1, tiled=True)]
  transfers between devices with their start and end apart: 5 -> 6, of which waited for: 3 -> 3; matrix products, arithmetic and copies ran while one was open for 24% -> 25% of each run, Pallas kernels for 0% -> 0%
where the time goes in v1:
time: 430 us; the launch traced here: 424 us
  waiting for transfers between devices  160 us (37%)
  other arithmetic  139 us (32%)
  blocking collectives  47.2 us (11%)
  local copies, waits for them, and re-layouts  45.6 us (11%)
  between operations  14.6 us (3%)
  matrix products  10.8 us (3%)
  starting transfers between devices  5.43 us (1%)
    all_gather x4, waiting for transfers between devices, prefix_2(): gathered = jax.tree.map(lambda a: lax.all_gather(a, axis), part)  160 us
    add x63, other arithmetic, combine(): late_sim + late_are * early_sim + late_aim * early_sre  54.8 us
    mul x2, other arithmetic, pole_power(): magnitude * jnp.cos(rotation * powers)  24.9 us
    reduce_sum x1, other arithmetic, local(): jnp.sum(norm_factor * (residue_re * state_re - residue_im * state_im), ax...  21.3 us
    slice x1, local copies, waits for them, and re-layouts, local(): sum_re = summed[:, :, :modes]  11 us
    reshape x1, local copies, waits for them, and re-layouts, local(): lifted = lifted.reshape(nblocks, block_len, 2 * modes * channels)  10.9 us
    dot_general x1, matrix products, local(): jnp.einsum('bts,bsk->btk', within, lifted, precision=lax.Precision.HIGHEST)  10.8 us
    reshape x1, local copies, waits for them, and re-layouts, local(): summed = summed.reshape(nblocks, block_len, 2 * modes, channels)  10.8 us
  transfers between devices with their start and end apart: 6, of which 3 were waited for; matrix products, arithmetic and copies ran while one was open for 25% of the time, Pallas kernels for 0%

profile of v1, /device:TPU:249, one launch (start us, length us, event | category | flops | bytes accessed | tf_op | source)
XLA Modules:
  0.0 424.2 jit_solution(8819647179601407285)
XLA Ops:
  6.5 1.3 stack.2
  7.9 4.0 all-to-all-start
  12.6 1.3 fusion.14
  15.8 9.8 %all_gather.41 = f32[2,4096]{1,0:T(2,128)S(1)} all-gather(f32[2,1024]{1,0:T(2,128)} %param.14), channel_id=1, replica_groups=mesh['dp'=4,'seq'=64] {'dp'}, dimensions={1}, use_global_device_ids=true | all-gather | bytes 40960 | tf_op jit(solution)/shard_map/all_gather | solution.py:49
  25.6 1.7 multiply_bitcast_fusion
  28.3 1.3 collective-permute-start
  29.7 9.4 %all_gather.39 = f32[3,3,4096]{2,1,0:T(4,128)S(1)} all-gather(f32[3,3,1024]{2,1,0:T(4,128)} %param.13), channel_id=1, replica_groups=mesh['dp'=4,'seq'=64] {'dp'}, dimensions={2}, use_global_device_ids=true | all-gather | bytes 184320 | tf_op jit(solution)/shard_map/all_gather | solution.py:48
  39.7 8.6 %fusion.6 = (f32[32,2,4096]{2,0,1:T(8,128)S(1)}, f32[32,2,4096]{2,0,1:T(8,128)S(1)}, f32[32,2,4096]{2,0,1:T(8,128)}, f32[32,2,4096]{2,0,1:T(8,128)}) fusion(f32[32]{0:T(128)S(1)} %iota_add_fusion, f32[2,4096]{1,0:T(2,128)S(1)} %bitcast.85, f32[2,4096]{1,0:T(2,128)S(1)} %get-tuple-element.234), kind=kLoop, calls=%fused_computation.32 | loop fusion | flops 2097152 | bytes 4259968 | tf_op jit(solution)/shard_map/mul | solution.py:37
  48.3 16.3 %cosine_multiply_fusion = (f32[32,2,4096]{2,1,0:T(2,128)}, f32[32,2,4096]{2,1,0:T(2,128)}) fusion(f32[2,4096]{1,0:T(2,128)S(1)} %get-tuple-element.233, f32[2,4096]{1,0:T(2,128)S(1)} %all_gather.41), kind=kLoop, calls=%fused_computation.37 | loop fusion | flops 1048576 | bytes 2162688 | tf_op jit(solution)/shard_map/mul | solution.py:37
  64.7 2.7 maximum_bitcast_fusion
  67.4 2.3 multiply_add_fusion
  70.0 1.7 copy-done.4
  71.7 1.1 copy-done.5
  72.8 3.9 broadcast_multiply_fusion.1
  76.7 9.7 %pad_maximum_fusion = f32[4,32,4,4096]{3,2,1,0:T(4,128)} fusion(f32[4,32,2,4096]{3,2,1,0:T(2,128)} %get-tuple-element.218, f32[4,32,2,4096]{3,2,1,0:T(2,128)S(1)} %get-tuple-element.217), kind=kLoop, calls=%fused_computation.14 | loop fusion | flops 2097152 | bytes 16777216 | tf_op jit(solution)/shard_map/concatenate | solution.py:79
  86.4 10.9 %reshape.169 = f32[4,32,16384]{2,1,0:T(8,128)} reshape(f32[4,32,4,4096]{3,2,1,0:T(4,128)} %pad_maximum_fusion) | data formatting | bytes 16777216 | tf_op jit(solution)/shard_map/reshape | solution.py:80
  97.3 10.8 %fusion.8 = f32[4,32,16384]{2,1,0:T(8,128)} fusion(f32[4,32,16384]{2,1,0:T(8,128)} %reshape.169, s32[4,32]{1,0:T(4,128)S(1)} %sub.35, pred[32,32]{1,0:T(8,128)(4,1)S(1)} %iota_compare_fusion), kind=kOutput, calls=%fused_computation.48 | convolution fusion | flops 805314560 | bytes 16778752 | tf_op jit(solution)/shard_map/bts,bsk->btk/dot_general | solution.py:84
  108.1 10.8 %reshape.170 = f32[4,32,4,4096]{3,2,1,0:T(4,128)} reshape(f32[4,32,16384]{2,1,0:T(8,128)} %fusion.8) | data formatting | bytes 16777216 | tf_op jit(solution)/shard_map/reshape | solution.py:85
  119.0 11.0 %fusion.15 = (f32[4,32,2,4096]{3,2,1,0:T(2,128)S(1)}, f32[4,32,2,4096]{3,2,1,0:T(2,128)}) fusion(f32[4,32,4,4096]{3,2,1,0:T(4,128)} %reshape.170), kind=kLoop, calls=%fused_computation.75 | loop fusion | bytes 16777216 | tf_op jit(solution)/shard_map/slice | solution.py:86
  130.0 7.8 %multiply_subtract_fusion = (f32[4,32,2,4096]{3,1,2,0:T(8,128)S(1)}, f32[4,32,2,4096]{3,1,2,0:T(8,128)S(1)}) fusion(f32[4,32,2,4096]{3,2,1,0:T(2,128)} %get-tuple-element.216, f32[4,32,2,4096]{3,2,1,0:T(2,128)S(1)} %get-tuple-element.215, f32[32,2,4096]{2,0,1:T(8,128)S(1)} %copy-done.3, f32[32,2,4096]{2,0,1:T(8,128)} %get-tuple-element.225), kind=kLoop, calls=%fused_computation.22 | loop fusion | flops 6291456 | bytes 18874368 | tf_op jit(solution)/shard_map/sub | solution.py:88
  137.9 2.0 copy-done.1
  140.0 1.1 copy-done.2
  141.5 7.9 %while.33 = (s32[]{:T(128)}, f32[2,4096]{1,0:T(2,128)S(1)}, f32[2,4096]{1,0:T(2,128)S(1)}, f32[4,2,4096]{2,1,0:T(2,128)S(1)}, f32[4,2,4096]{2,1,0:T(2,128)}, /*i...) while((s32[]{:T(128)}, f32[2,4096]{1,0:T(2,128)S(1)}, ...), condition=%wide.region_3.4_spmd.clone, body=%wide.region_2.3_spmd.clone.sunk | while | flops 114691 | bytes 393876 | solution.py:102
  150.7 9.0 %all_gather.40 = f32[4096]{0:T(1024)S(1)} all-gather(f32[1024]{0:T(1024)S(1)} %copy-done.10), channel_id=1, replica_groups=mesh['dp'=4,'seq'=64] {'dp'}, dimensions={0}, use_global_device_ids=true | all-gather | bytes 20480 | tf_op jit(solution)/shard_map/all_gather | solution.py:53
  159.7 9.6 %all_gather.42 = f32[2,4096]{1,0:T(2,128)S(1)} all-gather(f32[2,1024]{1,0:T(2,128)S(1)} %copy-done.8), channel_id=1, replica_groups=mesh['dp'=4,'seq'=64] {'dp'}, dimensions={1}, use_global_device_ids=true | all-gather | bytes 40960 | tf_op jit(solution)/shard_map/all_gather | solution.py:51
  169.3 9.4 %all_gather.51 = f32[2,4096]{1,0:T(2,128)S(1)} all-gather(f32[2,1024]{1,0:T(2,128)S(1)} %copy-done.9), channel_id=1, replica_groups=mesh['dp'=4,'seq'=64] {'dp'}, dimensions={1}, use_global_device_ids=true | all-gather | bytes 40960 | tf_op jit(solution)/shard_map/all_gather | solution.py:52
  178.8 4.3 %all-gather.17.cloned.1.call-done = f32[64,2,4096]{2,1,0:T(2,128)} async-done(((f32[1,2,4096]{2,1,0:T(2,128)}), f32[64,2,4096]{2,1,0:T(2,128)}) %all-gather.17.cloned.1.call-update) | async-done | bytes 2097168 | tf_op jit(solution)/shard_map/all_gather | solution.py:24
  183.1 77.7 %all-gather.13.cloned.1.call-done = f32[64,2,4096]{2,1,0:T(2,128)} async-done(((f32[1,2,4096]{2,1,0:T(2,128)}), f32[64,2,4096]{2,1,0:T(2,128)}) %all-gather.13.cloned.1.call-update) | async-done | bytes 2097168 | tf_op jit(solution)/shard_map/all_gather | solution.py:24
  260.8 77.6 %all-gather.19.cloned.1.call-done = f32[64,2,4096]{2,1,0:T(2,128)} async-done(((f32[1,2,4096]{2,1,0:T(2,128)}), f32[64,2,4096]{2,1,0:T(2,128)}) %all-gather.19.cloned.1.call-update) | async-done | bytes 2097168 | tf_op jit(solution)/shard_map/all_gather | solution.py:24
  338.5 56.2 %while.32 = (s32[]{:T(128)}, f32[2,4096]{1,0:T(2,128)S(1)}, f32[2,4096]{1,0:T(2,128)S(1)}, s32[]{:T(128)}, f32[64,2,4096]{2,1,0:T(2,128)}, /*index=5*/f32[64,2,4...) while((s32[]{:T(128)}, f32[2,4096]{1,0:T(2,128)S(1)}, ...), condition=%wide.region_5.6_spmd, body=%wide.region_4.5_spmd.sunk | while | flops 65541 | bytes 262291 | solution.py:32
  394.7 21.3 %multiply_reduce_fusion = f32[4,32,4096]{2,1,0:T(8,128)S(1)} fusion(f32[4,32,2,4096]{3,1,2,0:T(8,128)} %copy-done.2, f32[4,32,2,4096]{3,1,2,0:T(8,128)} %copy-done.1, f32[2,4096]{1,0:T(2,128)S(1)} %all_gather.51, f32[2,4096]{1,0:T(2,128)S(1)} %get-tuple-element.135, f32[2,4096]{1,0:T(2,128)S(1)} %get-tuple-element.134, f32[2,4096]{1,0:T(2,128)S(1)} %bitcast.86, ...), kind=kLoop, calls=%fused_computation.20 | loop fusion | flops 29884416 | bytes 13075968 | tf_op jit(solution)/shard_map/reduce_sum | solution.py:139
  416.1 1.6 fusion.5
  (133 shorter events, 67.7 us)
Async XLA Ops:
  7.9 17.7 %all-to-all-start = ((f32[4,2,1024]{2,1,0:T(2,128)}), f32[4,2,1024]{2,1,0:T(2,128)S(1)}, u32[]{:S(2)}, u32[]{:S(2)}) async-start(f32[4,2,1024]{2,1,0:T(2,128)} %stack.2), calls=%async_computation | async-start | bytes 65536 | tf_op jit(solution)/shard_map/all_to_all | solution.py:12
  11.9 166.9 %all-gather.15.cloned.1.call-start = ((), (), s32[]{:S(2)}) async-start(), calls=%async_computation.2 | async-start | bytes 2129920 | tf_op jit(solution)/shard_map/all_gather | solution.py:24
  27.3 155.8 %all-gather.17.cloned.1.call-start = ((), (), s32[]{:S(2)}) async-start(), calls=%async_computation.3 | async-start | bytes 2129920 | tf_op jit(solution)/shard_map/all_gather | solution.py:24
  28.3 36.3 %collective-permute-start = (bf16[3,1,2,4096]{3,2,0,1:T(2,128)(2,1)S(1)}, bf16[3,1,2,4096]{3,2,0,1:T(2,128)(2,1)S(1)}, u32[]{:S(2)}, u32[]{:S(2)}) collective-permute-start(bf16[3,1,2,4096]{3,2,0,1:T(2,128)(2,1)S(1)} %slice.69), channel_id=1, source_target_pairs={{0,1},{1,2},{2,3},{3,4},{4,5},{5,6},{6,7},{7,8},{8,9},{9,10},{10,1... | collective-permute-start | bytes 147464 | tf_op jit(solution)/shard_map/ppermute | solution.py:19
  64.6 196.2 %all-gather.13.cloned.1.call-start = ((), (), s32[]{:S(2)}) async-start(), calls=%async_computation.1 | async-start | bytes 2129920 | tf_op jit(solution)/shard_map/all_gather | solution.py:24
  69.7 7.0 %copy-start = (f32[3,128,4096]{2,1,0:T(8,128)}, f32[3,128,4096]{2,1,0:T(8,128)S(1)}, u32[]{:S(2)}) copy-start(f32[3,128,4096]{2,1,0:T(8,128)S(1)} %multiply_add_fusion) | copy-start | bytes 18874372
  69.7 2.0 copy-start.4
  69.7 3.1 copy-start.5
  119.0 11.1 %copy-start.3 = (f32[32,2,4096]{2,0,1:T(8,128)S(1)}, f32[32,2,4096]{2,0,1:T(8,128)}, u32[]{:S(2)}) copy-start(f32[32,2,4096]{2,0,1:T(8,128)} %get-tuple-element.224) | copy-start | bytes 3145732
  130.0 20.6 %copy-start.10 = (f32[1024]{0:T(1024)S(1)}, f32[1024]{0:T(1024)}, u32[]{:S(2)}) copy-start(f32[1024]{0:T(1024)} %param.18) | copy-start | bytes 12292
  130.0 29.7 %copy-start.8 = (f32[2,1024]{1,0:T(2,128)S(1)}, f32[2,1024]{1,0:T(2,128)}, u32[]{:S(2)}) copy-start(f32[2,1024]{1,0:T(2,128)} %param.16) | copy-start | bytes 24580
  130.0 39.3 %copy-start.9 = (f32[2,1024]{1,0:T(2,128)S(1)}, f32[2,1024]{1,0:T(2,128)}, u32[]{:S(2)}) copy-start(f32[2,1024]{1,0:T(2,128)} %param.17) | copy-start | bytes 24580
  137.9 2.0 copy-start.1
  137.9 3.3 copy-start.2
  149.4 0.6 copy-start.6
  149.4 0.7 copy-start.7
  150.1 188.4 %all-gather.19.cloned.1.call-start = ((), (), s32[]{:S(2)}) async-start(), calls=%async_computation.4 | async-start | bytes 2129920 | tf_op jit(solution)/shard_map/all_gather | solution.py:24
  394.7 21.4 %slice-start = ((s8[6291456]{0:T(1024)(128)(4,1)}), s8[4194304]{0:T(1024)(128)(4,1)S(1)}, s32[]{:S(2)}) async-start(s8[6291456]{0:T(1024)(128)(4,1)} %bitcast.76), calls=%async_computation.5 | async-start | bytes 8388608
  394.7 21.4 %slice-start.1 = ((s8[6291456]{0:T(1024)(128)(4,1)}), s8[2097152]{0:T(1024)(128)(4,1)S(1)}, s32[]{:S(2)}) async-start(s8[6291456]{0:T(1024)(128)(4,1)} %bitcast.76), calls=%async_computation.6 | async-start | bytes 4194304
Sparse Core Ops, SparseCore 0:
  27.4 77.8 all-gather.14
  108.1 74.9 all-gather.16
  185.9 74.9 all-gather.12
  263.5 74.9 all-gather.18
